TPU v7x, 32 devices: a whole 2x2x4 slice. The times are simulated.
32 devices in a mesh: gx: 2 (over y), gy: 4 (over x, core), gz: 4 (over z).
Axes of the slice: x: 2, y: 2, z: 4, core: 2. Of those that a mesh axis runs over, the one named last changes fastest.
Arguments:
- fluid_state: float32 [4, 32, 64, 512], P(None, 'gx', 'gy', 'gz'), may hold values from -6 to 6
- shell_disp: float32 [3, 32768], P(None, ('gy', 'gz')), may hold values from -6 to 6
- quad_weights: float32 [32, 32, 64], P(('gx', 'gy', 'gz')), may hold values from 0.25 to 1
- quad_elements: int32 [32, 32, 64], P(('gx', 'gy', 'gz')), may hold values from 0 to 32767
- owner_cells: int32 [32, 32, 64], P(('gx', 'gy', 'gz')), may hold values from 0 to 32767
- owner_counts: int32 [32, 32], P(('gx', 'gy', 'gz')), may hold values from 0 to 64, as said below
Outputs:
- fluid_out: float32 [4, 32, 64, 512], P(None, 'gx', 'gy', 'gz')
- shell_out: float32 [3, 32768], P(None, ('gy', 'gz'))
Inputs may be any that keep to these rules, and one draw needn't show every extreme that they name: `owner_counts`: some owner has 64 live records from every sender; some owner has none from some sender.
All inputs are finite; a program needn't handle non-finite values.
Results may differ from a plain program's by a relative error of at most 0.000023.
Values sent between devices are 32-bit elements; how exact they have to be, the bound alone decides.
A program may use at most 128 MiB of HBM per device.

v0:
```python
import jax
import jax.numpy as jnp
from jax import lax
from jax.sharding import PartitionSpec as P

ITERS = 2
advection = 0.2
penalty = 0.5
relaxation = 0.05


def with_halo(cells, sides, width):
    for axis, dim in sides:
        count = lax.axis_size(axis)
        ends = count - 1
        head = lax.slice_in_dim(cells, 0, width, axis=dim)
        tail = lax.slice_in_dim(cells, cells.shape[dim] - width, cells.shape[dim], axis=dim)
        cells = jnp.concatenate(
            [
                lax.ppermute(tail, axis, [(i, (i + 1) % count) for i in range(ends)]),
                cells,
                lax.ppermute(head, axis, [((i + 1) % count, i) for i in range(ends)]),
            ],
            axis=dim,
        )
    return cells


def smooth_axis(values, axis):
    length = values.shape[axis] - 2
    lower = lax.slice_in_dim(values, 0, length, axis=axis)
    middle = lax.slice_in_dim(values, 1, length + 1, axis=axis)
    upper = lax.slice_in_dim(values, 2, length + 2, axis=axis)
    return 0.25 * lower + 0.5 * middle + 0.25 * upper


def sweep_fluid(padded):
    smoothed = smooth_axis(smooth_axis(smooth_axis(padded, 1), 2), 3)
    center = padded[:, 1:-1, 1:-1, 1:-1]
    grad_x = 0.5 * (padded[:, 2:, 1:-1, 1:-1] - padded[:, :-2, 1:-1, 1:-1])
    grad_y = 0.5 * (padded[:, 1:-1, 2:, 1:-1] - padded[:, 1:-1, :-2, 1:-1])
    grad_z = 0.5 * (padded[:, 1:-1, 1:-1, 2:] - padded[:, 1:-1, 1:-1, :-2])
    convect = center[0:1] * grad_x + center[1:2] * grad_y + center[2:3] * grad_z
    updated = smoothed - advection * convect
    pressure_grad = jnp.stack([grad_x[3], grad_y[3], grad_z[3]])
    return jnp.concatenate([updated[0:3] - advection * pressure_grad, updated[3:4]], 0)


def on_device(fluid_state, shell_disp, quad_weights, quad_elements, owner_cells, owner_counts):
    slots = quad_weights.shape[2]
    elements = quad_elements[0]
    cells_local = owner_cells[0]
    slot_index = jnp.arange(slots, dtype=jnp.int32)[None, :]
    live_mask = (slot_index < owner_counts[0][:, None]).astype(jnp.float32)
    block_shape = fluid_state.shape
    for iteration in range(ITERS):
        padded = with_halo(fluid_state, (("gx", 1), ("gy", 2), ("gz", 3)), 1)
        halfway = sweep_fluid(padded)
        all_nodes = lax.all_gather(shell_disp, ("gy", "gz"), axis=1, tiled=True)
        shell_vel = all_nodes[:, elements]
        records = jnp.concatenate([shell_vel, quad_weights[0][None]], 0)
        received = lax.all_to_all(
            records, ("gx", "gy", "gz"), split_axis=1, concat_axis=1, tiled=True
        )
        flat_vel = halfway[0:3].reshape(3, -1)
        velocity = flat_vel[:, cells_local]
        traction = penalty * received[3][None] * (velocity - received[0:3]) * live_mask[None]
        forcing = jnp.zeros_like(flat_vel).at[:, cells_local].add(traction)
        forcing = forcing.reshape(3, block_shape[1], block_shape[2], block_shape[3])
        fluid_state = jnp.concatenate([halfway[0:3] - forcing, halfway[3:4]], 0)
        returned = lax.all_to_all(
            traction, ("gx", "gy", "gz"), split_axis=1, concat_axis=1, tiled=True
        )
        node_terms = jnp.zeros((3, all_nodes.shape[1]), jnp.float32).at[:, elements].add(returned)
        partial_loads = lax.psum_scatter(node_terms, ("gy", "gz"), scatter_dimension=1, tiled=True)
        node_loads = lax.psum(partial_loads, "gx")
        shell_disp = shell_disp + relaxation * node_loads
    return (fluid_state, shell_disp)


def solution(mesh):
    return jax.shard_map(
        on_device,
        mesh=mesh,
        in_specs=(
            P(None, "gx", "gy", "gz"),
            P(None, ("gy", "gz")),
            P(("gx", "gy", "gz"), None, None),
            P(("gx", "gy", "gz"), None, None),
            P(("gx", "gy", "gz"), None, None),
            P(("gx", "gy", "gz"), None),
        ),
        out_specs=(P(None, "gx", "gy", "gz"), P(None, ("gy", "gz"))),
        check_vma=False,
    )
```

profile of v0, /device:TPU:0, one launch (start us, length us, event | category | flops | bytes accessed | tf_op | source)
XLA Modules:
  0.0 1414.3 jit_solution(13298228462873777052)
XLA Ops:
  7.2 0.8 fusion.46
  8.0 4.9 collective-permute-start
  12.8 1.3 collective-permute-start.1
  15.0 1.1 copy.153
  16.1 359.1 %all_gather.6 = f32[3,32768]{0,1:T(8,128)} all-gather(f32[3,2048]{0,1:T(8,128)S(1)} %copy.153), channel_id=1, replica_groups=mesh['gx'=2,'gy'=4,'gz'=4] {'gy','gz'}, dimensions={1}, use_global_device_ids=true | all-gather | bytes 417792 | tf_op jit(solution)/shard_map/all_gather | solution.py:59
  375.3 11.2 gather_fusion
  387.7 5.4 all-to-all-start
  394.7 2.2 collective-permute-start.2
  396.9 1.3 collective-permute-start.3
  398.2 4.2 copy.142
  403.8 4.3 copy.141
  408.1 4.3 copy.143
  412.5 8.1 pad_maximum_fusion
  420.6 2.6 copy-done.1
  423.9 4.2 collective-permute-start.4
  428.0 1.7 collective-permute-start.5
  429.8 4.6 copy.145
  435.6 1.3 copy.144
  437.0 2.3 copy.146
  439.3 1.9 pad_maximum_fusion.2
  442.6 0.9 fusion.26
  444.3 8.7 copy.157
  453.0 13.3 gather_fusion.1
  466.3 1.6 copy.158
  468.0 1.4 copy.190
  469.4 18.6 %scatter_custom_fusion = f32[3,32768]{0,1:T(8,128)} fusion(s32[2048]{0:T(1024)} %copy-done.35, f32[2048,3]{1,0:T(8,128)} %bitcast.86, f32[]{:T(128)} %constant.10.clone.1), kind=kCustom, calls=%fused_computation.14 | custom fusion | flops 6144 | bytes 393728 | tf_op jit(solution)/shard_map/scatter-add | solution.py:68
  488.0 10.0 copy.161
  498.1 3.4 collective-permute-start.6
  501.5 1.3 collective-permute-start.7
  503.5 10.1 all-to-all-start.1
  514.5 2.2 collective-permute-start.8
  516.6 1.5 collective-permute-start.9
  518.2 4.3 copy.165
  522.5 0.8 reduce.1
  523.4 4.3 copy.164
  527.6 4.2 copy.166
  531.8 8.1 pad_maximum_fusion.1
  540.0 2.6 copy-done
  542.6 3.5 collective-permute-start.10
  546.2 1.3 collective-permute-start.11
  547.5 1.4 copy.191
  548.9 18.6 %scatter_custom_fusion.1 = f32[3,32768]{0,1:T(8,128)} fusion(s32[2048]{0:T(1024)} %copy-done.34, f32[2048,3]{1,0:T(8,128)} %bitcast.87, f32[]{:T(128)} %constant.10.clone.1), kind=kCustom, calls=%fused_computation.12 | custom fusion | flops 6144 | bytes 393728 | tf_op jit(solution)/shard_map/scatter-add | solution.py:74
  567.5 4.6 copy.168
  572.8 1.5 copy.167
  574.2 1.5 copy.169
  575.7 2.2 pad_maximum_fusion.3
  579.3 1.6 fusion.20
  581.1 168.3 %reduce-scatter.3.cloned.1.call-done = f32[3,2048]{0,1:T(8,128)} async-done(((f32[3,32768]{0,1:T(8,128)}), f32[3,2048]{0,1:T(8,128)}) %reduce-scatter.3.cloned.1.call-update) | async-done | bytes 24592 | tf_op jit(solution)/shard_map/reduce_scatter | solution.py:75
  749.3 28.5 %psum.14 = f32[3,2048]{0,1:T(8,128)S(1)} all-reduce(f32[3,2048]{0,1:T(8,128)} %reduce-scatter.3.cloned.1.call-done), channel_id=1, replica_groups=mesh['gx'=2,'gy'=4,'gz'=4] {'gx'}, use_global_device_ids=true, to_apply=%region_3.0 | all-reduce | flops 6144 | bytes 49152 | tf_op jit(solution)/shard_map/psum | solution.py:76
  777.9 353.5 %all_gather.7 = f32[3,32768]{0,1:T(8,128)} all-gather(f32[3,2048]{0,1:T(8,128)S(1)} %multiply_add_fusion.1), channel_id=1, replica_groups=mesh['gx'=2,'gy'=4,'gz'=4] {'gy','gz'}, dimensions={1}, use_global_device_ids=true | all-gather | bytes 417792 | tf_op jit(solution)/shard_map/all_gather | solution.py:59
  1131.4 11.2 gather_fusion.2
  1143.8 5.2 all-to-all-start.2
  1149.1 8.7 copy.182
  1157.8 11.2 gather_fusion.3
  1169.4 0.8 reduce.2
  1171.1 5.8 all-to-all-start.3
  1177.0 7.2 all-to-all-done.3
  1185.5 18.4 %scatter_custom_fusion.3 = f32[3,32768]{0,1:T(8,128)} fusion(s32[2048]{0:T(1024)} %copy-done.34, f32[2048,3]{1,0:T(8,128)S(1)} %bitcast.85, f32[]{:T(128)} %constant.10.clone.1), kind=kCustom, calls=%fused_computation.8 | custom fusion | flops 6144 | bytes 393728 | tf_op jit(solution)/shard_map/scatter-add | solution.py:74
  1204.3 21.6 %scatter_custom_fusion.2 = f32[3,32768]{0,1:T(8,128)} fusion(s32[2048]{0:T(1024)} %copy-done.35, f32[2048,3]{1,0:T(8,128)S(1)} %bitcast.84, f32[]{:T(128)} %constant.10.clone.1), kind=kCustom, calls=%fused_computation.10 | custom fusion | flops 6144 | bytes 393728 | tf_op jit(solution)/shard_map/scatter-add | solution.py:68
  1225.9 10.3 copy.186
  1236.3 0.8 pad_maximum_fusion.25
  1237.2 140.6 %reduce-scatter.5.cloned.1.call-done = f32[3,2048]{0,1:T(8,128)} async-done(((f32[3,32768]{0,1:T(8,128)}), f32[3,2048]{0,1:T(8,128)}) %reduce-scatter.5.cloned.1.call-update) | async-done | bytes 24592 | tf_op jit(solution)/shard_map/reduce_scatter | solution.py:75
  1377.7 28.5 %psum.15 = f32[3,2048]{0,1:T(8,128)S(1)} all-reduce(f32[3,2048]{0,1:T(8,128)} %reduce-scatter.5.cloned.1.call-done), channel_id=1, replica_groups=mesh['gx'=2,'gy'=4,'gz'=4] {'gx'}, use_global_device_ids=true, to_apply=%region_7.0 | all-reduce | flops 6144 | bytes 49152 | tf_op jit(solution)/shard_map/psum | solution.py:76
  1406.3 0.9 copy.189
  (164 shorter events, 17.6 us)
Async XLA Ops:
  8.0 386.0 %collective-permute-start = (f32[4,1,16,128]{3,2,1,0:T(8,128)S(1)}, f32[4,1,16,128]{3,2,1,0:T(8,128)S(1)}, u32[]{:S(2)}, u32[]{:S(2)}) collective-permute-start(f32[4,1,16,128]{3,2,1,0:T(8,128)S(1)} %get-tuple-element.36), channel_id=1, source_target_pairs={{0,16},{1,17},{2,18},{3,19},{4,20},{5,21},{6,22},{7,23},{8,24},{9,... | collective-permute-start | bytes 98312 | tf_op jit(solution)/shard_map/ppermute | solution.py:20
  12.8 381.2 %collective-permute-start.1 = (f32[4,1,16,128]{3,2,1,0:T(8,128)S(1)}, f32[4,1,16,128]{3,2,1,0:T(8,128)S(1)}, u32[]{:S(2)}, u32[]{:S(2)}) collective-permute-start(f32[4,1,16,128]{3,2,1,0:T(8,128)S(1)} %get-tuple-element.35), channel_id=1, source_target_pairs={{16,0},{17,1},{18,2},{19,3},{20,4},{21,5},{22,6},{23,7},{24,8},{25... | collective-permute-start | bytes 98312 | tf_op jit(solution)/shard_map/ppermute | solution.py:22
  14.9 360.3 %copy-start.34 = (s32[2048]{0:T(1024)}, s32[2048]{0:T(1024)S(1)}, u32[]{:S(2)}) copy-start(s32[2048]{0:T(1024)S(1)} %reshape.111) | copy-start | bytes 24580
  15.0 360.3 %copy-start.15 = (s32[2048]{0:T(1024)}, s32[2048]{0:T(1024)S(1)}, u32[]{:S(2)}) copy-start(s32[2048]{0:T(1024)S(1)} %broadcast_clamp_fusion.1) | copy-start | bytes 24580
  16.1 370.8 %copy-start.32 = (f32[1,32,64]{2,1,0:T(8,128)S(1)}, f32[1,32,64]{2,1,0:T(8,128)}, u32[]{:S(2)}) copy-start(f32[1,32,64]{2,1,0:T(8,128)} %param.8) | copy-start | bytes 24580
  16.1 377.0 %copy-start.5 = (f32[4,16,16,128]{3,2,1,0:T(8,128)S(1)}, f32[4,16,16,128]{3,2,1,0:T(8,128)}, u32[]{:S(2)}) copy-start(f32[4,16,16,128]{3,2,1,0:T(8,128)} %param.6) | copy-start | bytes 1572868
  16.1 377.7 %copy-start.36 = (s32[1,32,64]{2,1,0:T(8,128)S(1)}, s32[1,32,64]{2,1,0:T(8,128)}, u32[]{:S(2)}) copy-start(s32[1,32,64]{2,1,0:T(8,128)} %param.10) | copy-start | bytes 24580
  16.1 377.7 %copy-start.37 = (s32[1,32]{1,0:T(1,128)S(1)}, s32[1,32]{1,0:T(1,128)}, u32[]{:S(2)}) copy-start(s32[1,32]{1,0:T(1,128)} %param.11) | copy-start | bytes 388
  387.7 14.7 %all-to-all-start = ((f32[32,1,256]{2,1,0:T(1,128)}), f32[32,1,256]{2,1,0:T(1,128)S(1)}, u32[]{:S(2)}, u32[]{:S(2)}) async-start(f32[32,1,256]{2,1,0:T(1,128)} %reshape.189), calls=%async_computation | async-start | bytes 65536 | tf_op jit(solution)/shard_map/all_to_all | solution.py:62
  393.9 8.4 copy-start.35
  393.9 2.9 copy-start.28
  394.0 0.6 copy-start.30
  394.6 13.5 copy-start.9
  394.7 9.2 collective-permute-start.2
  396.9 11.2 collective-permute-start.3
  398.2 54.8 %copy-start.17 = (s32[2048]{0:T(1024)}, s32[2048]{0:T(1024)S(1)}, u32[]{:S(2)}) copy-start(s32[2048]{0:T(1024)S(1)} %broadcast_clamp_fusion) | copy-start | bytes 24580
  403.8 8.7 copy-start.11
  420.6 2.6 copy-start.1
  423.9 11.8 collective-permute-start.4
  428.0 9.0 collective-permute-start.5
  441.2 1.2 copy-start.2
  441.2 1.3 copy-start.10
  441.2 1.3 copy-start.13
  441.2 1.4 copy-start.14
  441.2 1.3 copy-start.21
  441.2 1.3 copy-start.23
  441.2 1.3 copy-start.29
  441.3 1.3 copy-start.31
  443.4 0.8 copy-start.7
  444.3 23.6 %copy-start.12 = (f32[32,4,64]{2,1,0:T(4,128)S(1)}, f32[32,4,64]{2,1,0:T(4,128)}, u32[]{:S(2)}) copy-start(f32[32,4,64]{2,1,0:T(4,128)} %copy-done.11) | copy-start | bytes 98308
  488.0 10.0 copy-start.8
  498.1 15.6 %collective-permute-start.6 = (f32[4,1,16,128]{3,2,1,0:T(8,128)S(1)}, f32[4,1,16,128]{3,2,1,0:T(8,128)S(1)}, u32[]{:S(2)}, u32[]{:S(2)}) collective-permute-start(f32[4,1,16,128]{3,2,1,0:T(8,128)S(1)} %get-tuple-element.30), channel_id=1, source_target_pairs={{0,16},{1,17},{2,18},{3,19},{4,20},{5,21},{6,22},{7,23},{8,24},{9,... | collective-permute-start | bytes 98312 | tf_op jit(solution)/shard_map/ppermute | solution.py:20
  501.5 12.3 collective-permute-start.7
  503.5 19.0 %all-to-all-start.1 = ((f32[32,1,192]{2,1,0:T(1,128)}), f32[32,1,192]{2,1,0:T(1,128)S(1)}, u32[]{:S(2)}, u32[]{:S(2)}) async-start(f32[32,1,192]{2,1,0:T(1,128)} %reshape.191), calls=%async_computation.1 | async-start | bytes 65536 | tf_op jit(solution)/shard_map/all_to_all | solution.py:71
  513.7 235.7 %reduce-scatter.3.cloned.1.call-start = ((), (), s32[]{:S(2)}) async-start(), calls=%async_computation.6 | async-start | bytes 17825792 | tf_op jit(solution)/shard_map/reduce_scatter | solution.py:75
  513.7 13.9 copy-start.24
  513.7 0.6 copy-start.26
  514.5 8.9 collective-permute-start.8
  516.6 11.0 collective-permute-start.9
  527.6 12.3 copy-start.19
  540.0 2.6 copy-start
  542.6 30.2 %collective-permute-start.10 = (f32[4,18,18,1]{2,1,3,0:T(8,128)S(1)}, f32[4,18,18,1]{2,1,3,0:T(8,128)S(1)}, u32[]{:S(2)}, u32[]{:S(2)}) collective-permute-start(f32[4,18,18,1]{2,1,3,0:T(8,128)S(1)} %get-tuple-element.22), channel_id=1, source_target_pairs={{0,1},{1,2},{2,3},{4,5},{5,6},{6,7},{8,9},{9,10},{10,11},{12,13},{... | collective-permute-start | bytes 15560 | tf_op jit(solution)/shard_map/ppermute | solution.py:20
  546.2 28.1 %collective-permute-start.11 = (f32[4,18,18,1]{2,1,3,0:T(8,128)S(1)}, f32[4,18,18,1]{2,1,3,0:T(8,128)S(1)}, u32[]{:S(2)}, u32[]{:S(2)}) collective-permute-start(f32[4,18,18,1]{2,1,3,0:T(8,128)S(1)} %get-tuple-element.23), channel_id=1, source_target_pairs={{1,0},{2,1},{3,2},{5,4},{6,5},{7,6},{9,8},{10,9},{11,10},{13,12},{... | collective-permute-start | bytes 15560 | tf_op jit(solution)/shard_map/ppermute | solution.py:22
  567.5 4.6 copy-start.20
  577.9 1.2 copy-start.3
  577.9 1.4 copy-start.4
  577.9 1.4 copy-start.22
  577.9 1.4 copy-start.25
  577.9 1.4 copy-start.27
  777.9 353.5 %copy-start.16 = (s32[2048]{0:T(1024)S(1)}, s32[2048]{0:T(1024)}, u32[]{:S(2)}) copy-start(s32[2048]{0:T(1024)} %copy-done.15) | copy-start | bytes 24580
  777.9 365.1 %copy-start.33 = (f32[1,32,64]{2,1,0:T(8,128)S(1)}, f32[1,32,64]{2,1,0:T(8,128)}, u32[]{:S(2)}) copy-start(f32[1,32,64]{2,1,0:T(8,128)} %param.8) | copy-start | bytes 24580
  777.9 371.1 %copy-start.6 = (f32[4,16,16,128]{3,2,1,0:T(8,128)S(1)}, f32[4,16,16,128]{3,2,1,0:T(8,128)}, u32[]{:S(2)}) copy-start(f32[4,16,16,128]{3,2,1,0:T(8,128)} %get-tuple-element.14) | copy-start | bytes 1572868
  1143.8 25.6 %all-to-all-start.2 = ((f32[32,1,256]{2,1,0:T(1,128)}), f32[32,1,256]{2,1,0:T(1,128)S(1)}, u32[]{:S(2)}, u32[]{:S(2)}) async-start(f32[32,1,256]{2,1,0:T(1,128)} %reshape.193), calls=%async_computation.3 | async-start | bytes 65536 | tf_op jit(solution)/shard_map/all_to_all | solution.py:62
  1149.1 8.7 copy-start.18
  1171.1 13.1 all-to-all-start.3
  1176.9 200.8 %reduce-scatter.5.cloned.1.call-start = ((), (), s32[]{:S(2)}) async-start(), calls=%async_computation.7 | async-start | bytes 17825792 | tf_op jit(solution)/shard_map/reduce_scatter | solution.py:75
Sparse Core Ops, SparseCore 0:
  567.6 181.6 reduce-scatter.2
  1204.0 173.6 reduce-scatter.4
where the time goes:
time: 1420 us; the launch traced here: 1410 us
  blocking collectives  770 us (54%)
  waiting for transfers between devices  316 us (22%)
  local copies, waits for them, and re-layouts  151 us (11%)
  other arithmetic  107 us (8%)
  starting transfers between devices  55.2 us (4%)
  between operations  15.2 us (1%)
    all_gather x2, blocking collectives, on_device(): all_nodes = lax.all_gather(shell_disp, ('gy', 'gz'), axis=1, tiled=True)  713 us
    reduce_scatter x2, waiting for transfers between devices, on_device(): lax.psum_scatter(node_terms, ('gy', 'gz'), scatter_dimension=1, tiled=True)  309 us
    psum x2, blocking collectives, on_device(): node_loads = lax.psum(partial_loads, 'gx')  56.9 us
    scatter-add x2, other arithmetic, on_device(): forcing = jnp.zeros_like(flat_vel).at[:, cells_local].add(traction)  40.2 us
    scatter-add x2, other arithmetic, on_device(): jnp.zeros((3, all_nodes.shape[1]), jnp.float32).at[:, elements]  37 us
  transfers between devices with their start and end apart: 18, of which 3 were waited for; matrix products, arithmetic and copies ran while one was open for 9% of the time, Pallas kernels for 0%

commit v1 on v0

--- a/solution.py
+++ b/solution.py
@@ -7,6 +7,17 @@
 advection = 0.2
 penalty = 0.5
 relaxation = 0.05
+
+
+def collect(x, axis, dim):
+    ways = lax.axis_size(axis)
+    pieces = [x]
+    for far in range(1, ways):
+        pieces.append(
+            lax.ppermute(pieces[far - 1], axis, [(d, (d - 1) % ways) for d in range(ways)])
+        )
+    line = jnp.concatenate(pieces, axis=dim)
+    return jnp.roll(line, lax.axis_index(axis) * x.shape[dim], axis=dim)
 
 
 def with_halo(cells, sides, width):
@@ -56,7 +67,7 @@
     for iteration in range(ITERS):
         padded = with_halo(fluid_state, (("gx", 1), ("gy", 2), ("gz", 3)), 1)
         halfway = sweep_fluid(padded)
-        all_nodes = lax.all_gather(shell_disp, ("gy", "gz"), axis=1, tiled=True)
+        all_nodes = collect(shell_disp, ("gy", "gz"), 1)
         shell_vel = all_nodes[:, elements]
         records = jnp.concatenate([shell_vel, quad_weights[0][None]], 0)
         received = lax.all_to_all(

time: 1420 us -> 890 us (0.63)
  blocking collectives: 770 us -> 56.9 us
  starting transfers between devices: 55.2 us -> 170 us
  waiting for transfers between devices: 316 us -> 363 us
    all_gather x2 -> x0, blocking collectives: 713 us -> none  [on_device(): all_nodes = lax.all_gather(shell_disp, ('gy', 'gz'), axis=1, tiled=True)]
    ppermute x0 -> x30, starting transfers between devices: none -> 119 us  [collect(): lax.ppermute(pieces[far - 1], axis, [(d, (d - 1) % ways) for d in range(w...]
    ppermute x0 -> x30, waiting for transfers between devices: none -> 42.5 us  [collect(): lax.ppermute(pieces[far - 1], axis, [(d, (d - 1) % ways) for d in range(w...]
    unnamed x92 -> x98, local copies, waits for them, and re-layouts: 14.3 us -> 36.4 us
  transfers between devices with their start and end apart: 18 -> 48, of which waited for: 3 -> 29; matrix products, arithmetic and copies ran while one was open for 9% -> 18% of each run, Pallas kernels for 0% -> 0%
where the time goes in v1:
time: 890 us; the launch traced here: 880 us
  waiting for transfers between devices  363 us (41%)
  starting transfers between devices  170 us (19%)
  local copies, waits for them, and re-layouts  164 us (18%)
  other arithmetic  111 us (12%)
  blocking collectives  56.9 us (6%)
  between operations  15.2 us (2%)
    reduce_scatter x2, waiting for transfers between devices, on_device(): lax.psum_scatter(node_terms, ('gy', 'gz'), scatter_dimension=1, tiled=True)  313 us
    ppermute x30, starting transfers between devices, collect(): lax.ppermute(pieces[far - 1], axis, [(d, (d - 1) % ways) for d in range(w...  119 us
    psum x2, blocking collectives, on_device(): node_loads = lax.psum(partial_loads, 'gx')  56.9 us
    ppermute x30, waiting for transfers between devices, collect(): lax.ppermute(pieces[far - 1], axis, [(d, (d - 1) % ways) for d in range(w...  42.5 us
    scatter-add x2, other arithmetic, on_device(): forcing = jnp.zeros_like(flat_vel).at[:, cells_local].add(traction)  39.9 us
    scatter-add x2, other arithmetic, on_device(): jnp.zeros((3, all_nodes.shape[1]), jnp.float32).at[:, elements]  36.8 us
    unnamed x98, local copies, waits for them, and re-layouts  36.4 us
    gather x4, local copies, waits for them, and re-layouts, on_device(): shell_vel = all_nodes[:, elements]  24.2 us
  transfers between devices with their start and end apart: 48, of which 29 were waited for; matrix products, arithmetic and copies ran while one was open for 18% of the time, Pallas kernels for 0%

profile of v1, /device:TPU:0, one launch (start us, length us, event | category | flops | bytes accessed | tf_op | source)
XLA Modules:
  0.0 880.2 jit_solution(3950208234733368805)
XLA Ops:
  8.0 4.9 collective-permute-start
  14.1 3.7 collective-permute-start.6
  28.0 4.2 copy.153
  38.4 4.2 copy.152
  42.7 4.4 copy.154
  47.0 8.1 pad_maximum_fusion
  55.2 2.7 copy-done.1
  57.9 4.6 copy.156
  67.0 3.9 collective-permute-start.9
  80.6 3.6 collective-permute-start.11
  85.7 4.4 collective-permute-start.12
  91.8 4.4 collective-permute-start.13
  97.8 4.4 collective-permute-start.14
  103.8 4.4 collective-permute-start.15
  109.9 4.4 collective-permute-start.16
  115.9 4.4 collective-permute-start.17
  122.0 4.4 collective-permute-start.18
  128.0 4.4 collective-permute-start.19
  134.0 4.4 collective-permute-start.20
  141.0 8.5 copy.214
  149.4 11.2 %gather_fusion = f32[2048,3]{1,0:T(8,128)S(1)} fusion(f32[3,32768]{0,1:T(8,128)} %copy.214, s32[2048]{0:T(1024)S(1)} %get-tuple-element.44), kind=kCustom, calls=%fused_computation | custom fusion | bytes 57344 | tf_op jit(solution)/shard_map/gather | solution.py:71
  161.9 7.3 all-to-all-start
  169.3 8.7 copy.168
  178.0 11.2 %gather_fusion.1 = f32[2048,3]{1,0:T(8,128)S(1)} fusion(f32[3,32768]{0,1:T(8,128)} %bitcast.78, s32[2048]{0:T(1024)S(1)} %get-tuple-element.43), kind=kCustom, calls=%fused_computation.1 | custom fusion | bytes 57344 | tf_op jit(solution)/shard_map/gather | solution.py:77
  191.6 18.3 %scatter_custom_fusion = f32[3,32768]{0,1:T(8,128)} fusion(s32[2048]{0:T(1024)S(1)} %reshape.143, f32[2048,3]{1,0:T(8,128)S(1)} %bitcast.86, f32[]{:T(128)} %constant.11.clone.1), kind=kCustom, calls=%fused_computation.14 | custom fusion | flops 6144 | bytes 393220 | tf_op jit(solution)/shard_map/scatter-add | solution.py:79
  209.8 10.0 %copy.172 = f32[3,16,16,128]{3,2,1,0:T(8,128)S(1)} copy(f32[3,16,16,128]{0,3,2,1:T(8,128)} %bitcast.77) | data formatting | bytes 786432 | tf_op jit(solution)/shard_map/reshape | solution.py:80
  219.9 3.8 collective-permute-start.21
  225.8 6.7 all-to-all-start.1
  236.9 4.2 copy.176
  241.9 4.2 copy.175
  246.2 4.3 copy.177
  250.5 8.1 pad_maximum_fusion.1
  258.7 2.7 copy-done
  261.4 3.5 collective-permute-start.25
  266.8 18.4 %scatter_custom_fusion.1 = f32[3,32768]{0,1:T(8,128)} fusion(s32[2048]{0:T(1024)} %copy-done.24, f32[2048,3]{1,0:T(8,128)S(1)} %bitcast.87, f32[]{:T(128)} %constant.11.clone.1), kind=kCustom, calls=%fused_computation.12 | custom fusion | flops 6144 | bytes 393728 | tf_op jit(solution)/shard_map/scatter-add | solution.py:85
  285.2 4.6 copy.179
  295.2 172.5 %reduce-scatter.3.cloned.1.call-done = f32[3,2048]{0,1:T(8,128)} async-done(((f32[3,32768]{0,1:T(8,128)}), f32[3,2048]{0,1:T(8,128)}) %reduce-scatter.3.cloned.1.call-update) | async-done | bytes 24592 | tf_op jit(solution)/shard_map/reduce_scatter | solution.py:86
  467.7 28.4 %psum.14 = f32[3,2048]{0,1:T(8,128)S(1)} all-reduce(f32[3,2048]{0,1:T(8,128)} %reduce-scatter.3.cloned.1.call-done), channel_id=1, replica_groups=mesh['gx'=2,'gy'=4,'gz'=4] {'gx'}, use_global_device_ids=true, to_apply=%region_3.5 | all-reduce | flops 6144 | bytes 49152 | tf_op jit(solution)/shard_map/psum | solution.py:87
  501.7 3.8 collective-permute-start.28
  507.2 4.4 collective-permute-start.29
  513.2 4.4 collective-permute-start.30
  519.2 4.4 collective-permute-start.31
  525.3 4.4 collective-permute-start.32
  531.3 4.4 collective-permute-start.33
  537.5 4.6 collective-permute-start.34
  543.7 4.4 collective-permute-start.35
  549.7 4.4 collective-permute-start.36
  555.8 4.4 collective-permute-start.37
  561.8 4.4 collective-permute-start.38
  567.9 4.4 collective-permute-start.39
  574.1 4.6 collective-permute-start.40
  580.2 4.6 collective-permute-start.41
  587.4 8.5 copy.218
  595.9 12.2 %gather_fusion.2 = f32[2048,3]{1,0:T(8,128)S(1)} fusion(f32[3,32768]{0,1:T(8,128)} %copy.218, s32[2048]{0:T(1024)} %copy-done.11), kind=kCustom, calls=%fused_computation.2 | custom fusion | bytes 57344 | tf_op jit(solution)/shard_map/gather | solution.py:71
  609.9 4.8 all-to-all-start.2
  614.8 8.7 copy.196
  623.5 11.2 %gather_fusion.3 = f32[2048,3]{1,0:T(8,128)S(1)} fusion(f32[3,32768]{0,1:T(8,128)} %bitcast.79, s32[2048]{0:T(1024)S(1)} %copy-done.10), kind=kCustom, calls=%fused_computation.3 | custom fusion | bytes 57344 | tf_op jit(solution)/shard_map/gather | solution.py:77
  636.8 5.8 all-to-all-start.3
  642.7 7.2 all-to-all-done.3
  651.3 18.4 %scatter_custom_fusion.3 = f32[3,32768]{0,1:T(8,128)} fusion(s32[2048]{0:T(1024)} %copy-done.24, f32[2048,3]{1,0:T(8,128)S(1)} %bitcast.85, f32[]{:T(128)} %constant.11.clone.1), kind=kCustom, calls=%fused_computation.8 | custom fusion | flops 6144 | bytes 393728 | tf_op jit(solution)/shard_map/scatter-add | solution.py:85
  670.1 21.6 %scatter_custom_fusion.2 = f32[3,32768]{0,1:T(8,128)} fusion(s32[2048]{0:T(1024)} %copy-done.23, f32[2048,3]{1,0:T(8,128)S(1)} %bitcast.84, f32[]{:T(128)} %constant.11.clone.1), kind=kCustom, calls=%fused_computation.10 | custom fusion | flops 6144 | bytes 393728 | tf_op jit(solution)/shard_map/scatter-add | solution.py:79
  691.7 10.3 %copy.200 = f32[3,16,16,128]{3,2,1,0:T(8,128)S(1)} copy(f32[3,16,16,128]{0,3,2,1:T(8,128)} %bitcast.76) | data formatting | bytes 786432 | tf_op jit(solution)/shard_map/reshape | solution.py:80
  703.0 140.6 %reduce-scatter.5.cloned.1.call-done = f32[3,2048]{0,1:T(8,128)} async-done(((f32[3,32768]{0,1:T(8,128)}), f32[3,2048]{0,1:T(8,128)}) %reduce-scatter.5.cloned.1.call-update) | async-done | bytes 24592 | tf_op jit(solution)/shard_map/reduce_scatter | solution.py:86
  843.5 28.5 %psum.15 = f32[3,2048]{0,1:T(8,128)S(1)} all-reduce(f32[3,2048]{0,1:T(8,128)} %reduce-scatter.5.cloned.1.call-done), channel_id=1, replica_groups=mesh['gx'=2,'gy'=4,'gz'=4] {'gx'}, use_global_device_ids=true, to_apply=%region_7.9 | all-reduce | flops 6144 | bytes 49152 | tf_op jit(solution)/shard_map/psum | solution.py:87
  (232 shorter events, 104.2 us)
Async XLA Ops:
  8.0 18.3 %collective-permute-start = (f32[4,1,16,128]{3,2,1,0:T(8,128)S(1)}, f32[4,1,16,128]{3,2,1,0:T(8,128)S(1)}, u32[]{:S(2)}, u32[]{:S(2)}) collective-permute-start(f32[4,1,16,128]{3,2,1,0:T(8,128)S(1)} %get-tuple-element.37), channel_id=1, source_target_pairs={{0,16},{1,17},{2,18},{3,19},{4,20},{5,21},{6,22},{7,23},{8,24},{9,... | collective-permute-start | bytes 98312 | tf_op jit(solution)/shard_map/ppermute | solution.py:31
  12.8 14.5 %collective-permute-start.1 = (f32[4,1,16,128]{3,2,1,0:T(8,128)S(1)}, f32[4,1,16,128]{3,2,1,0:T(8,128)S(1)}, u32[]{:S(2)}, u32[]{:S(2)}) collective-permute-start(f32[4,1,16,128]{3,2,1,0:T(8,128)S(1)} %get-tuple-element.36), channel_id=1, source_target_pairs={{16,0},{17,1},{18,2},{19,3},{20,4},{21,5},{22,6},{23,7},{24,8},{25... | collective-permute-start | bytes 98312 | tf_op jit(solution)/shard_map/ppermute | solution.py:33
  14.1 11.3 %collective-permute-start.6 = (f32[3,2048]{1,0:T(4,128)}, f32[3,2048]{1,0:T(4,128)S(1)}, u32[]{:S(2)}, u32[]{:S(2)}) collective-permute-start(f32[3,2048]{1,0:T(4,128)} %param.9), channel_id=1, source_target_pairs={{0,15},{1,0},{2,1},{3,2},{4,3},{5,4},{6,5},{7,6},{8,7},{9,8},{10,9... | collective-permute-start | bytes 73736 | tf_op jit(solution)/shard_map/ppermute | solution.py:17
  21.8 20.9 %copy-start.24 = (s32[2048]{0:T(1024)}, s32[2048]{0:T(1024)S(1)}, u32[]{:S(2)}) copy-start(s32[2048]{0:T(1024)S(1)} %reshape.111) | copy-start | bytes 24580
  22.6 169.0 %copy-start.23 = (s32[2048]{0:T(1024)}, s32[2048]{0:T(1024)S(1)}, u32[]{:S(2)}) copy-start(s32[2048]{0:T(1024)S(1)} %reshape.143) | copy-start | bytes 24580
  22.6 126.9 %copy-start.11 = (s32[2048]{0:T(1024)}, s32[2048]{0:T(1024)S(1)}, u32[]{:S(2)}) copy-start(s32[2048]{0:T(1024)S(1)} %get-tuple-element.44) | copy-start | bytes 24580
  22.6 155.4 %copy-start.9 = (s32[2048]{0:T(1024)}, s32[2048]{0:T(1024)S(1)}, u32[]{:S(2)}) copy-start(s32[2048]{0:T(1024)S(1)} %get-tuple-element.43) | copy-start | bytes 24580
  25.4 10.3 %collective-permute-start.7 = (f32[3,2048]{1,0:T(4,128)S(1)}, f32[3,2048]{1,0:T(4,128)S(1)}, u32[]{:S(2)}, u32[]{:S(2)}) collective-permute-start(f32[3,2048]{1,0:T(4,128)S(1)} %collective-permute-done.6), channel_id=1, source_target_pairs={{0,15},{1,0},{2,1},{3,2},{4,3},{5,4},{6,5},{7,6},{8,7},{9,8},{10,9... | collective-permute-start | bytes 73736 | tf_op jit(solution)/shard_map/ppermute | solution.py:17
  28.0 14.7 %copy-start.4 = (f32[4,18,16,128]{3,2,1,0:T(8,128)}, f32[4,18,16,128]{3,2,1,0:T(8,128)S(1)}, u32[]{:S(2)}) copy-start(f32[4,18,16,128]{3,2,1,0:T(8,128)S(1)} %constant_dynamic-update-slice_fusion) | copy-start | bytes 1769476
  32.2 6.2 collective-permute-start.2
  34.4 8.2 collective-permute-start.3
  35.8 31.2 %collective-permute-start.8 = (f32[3,2048]{1,0:T(4,128)S(1)}, f32[3,2048]{1,0:T(4,128)}, u32[]{:S(2)}, u32[]{:S(2)}) collective-permute-start(f32[3,2048]{1,0:T(4,128)S(1)} %collective-permute-done.7), channel_id=1, source_target_pairs={{0,15},{1,0},{2,1},{3,2},{4,3},{5,4},{6,5},{7,6},{8,7},{9,8},{10,9... | collective-permute-start | bytes 73736 | tf_op jit(solution)/shard_map/ppermute | solution.py:17
  55.2 2.7 copy-start.1
  62.4 9.9 %collective-permute-start.4 = (f32[4,18,18,1]{2,1,3,0:T(8,128)S(1)}, f32[4,18,18,1]{2,1,3,0:T(8,128)S(1)}, u32[]{:S(2)}, u32[]{:S(2)}) collective-permute-start(f32[4,18,18,1]{2,1,3,0:T(8,128)S(1)} %get-tuple-element.25), channel_id=1, source_target_pairs={{0,1},{1,2},{2,3},{4,5},{5,6},{6,7},{8,9},{9,10},{10,11},{12,13},{... | collective-permute-start | bytes 15560 | tf_op jit(solution)/shard_map/ppermute | solution.py:31
  64.4 8.5 collective-permute-start.5
  67.0 9.4 %collective-permute-start.9 = (f32[3,2048]{1,0:T(4,128)}, f32[3,2048]{1,0:T(4,128)}, u32[]{:S(2)}, u32[]{:S(2)}) collective-permute-start(f32[3,2048]{1,0:T(4,128)} %collective-permute-done.8), channel_id=1, source_target_pairs={{0,15},{1,0},{2,1},{3,2},{4,3},{5,4},{6,5},{7,6},{8,7},{9,8},{10,9... | collective-permute-start | bytes 73736 | tf_op jit(solution)/shard_map/ppermute | solution.py:17
  74.2 1.2 copy-start.5
  74.2 1.2 copy-start.7
  74.2 1.2 copy-start.12
  74.5 3.4 copy-start.6
  76.4 4.2 collective-permute-start.10
  80.6 5.2 collective-permute-start.11
  85.7 6.0 collective-permute-start.12
  91.8 6.0 collective-permute-start.13
  97.8 6.0 collective-permute-start.14
  103.8 6.0 collective-permute-start.15
  109.9 6.0 collective-permute-start.16
  115.9 6.0 collective-permute-start.17
  122.0 6.0 collective-permute-start.18
  128.0 6.0 collective-permute-start.19
  134.0 6.0 collective-permute-start.20
  141.0 20.1 %copy-start.22 = (f32[1,32,64]{2,1,0:T(8,128)S(1)}, f32[1,32,64]{2,1,0:T(8,128)}, u32[]{:S(2)}) copy-start(f32[1,32,64]{2,1,0:T(8,128)} %param.10) | copy-start | bytes 24580
  161.9 27.7 %all-to-all-start = ((f32[32,1,256]{2,1,0:T(1,128)}), f32[32,1,256]{2,1,0:T(1,128)S(1)}, u32[]{:S(2)}, u32[]{:S(2)}) async-start(f32[32,1,256]{2,1,0:T(1,128)} %reshape.189), calls=%async_computation | async-start | bytes 65536 | tf_op jit(solution)/shard_map/all_to_all | solution.py:73
  219.9 12.6 %collective-permute-start.21 = (f32[4,1,16,128]{3,2,1,0:T(8,128)S(1)}, f32[4,1,16,128]{3,2,1,0:T(8,128)S(1)}, u32[]{:S(2)}, u32[]{:S(2)}) collective-permute-start(f32[4,1,16,128]{3,2,1,0:T(8,128)S(1)} %get-tuple-element.31), channel_id=1, source_target_pairs={{0,16},{1,17},{2,18},{3,19},{4,20},{5,21},{6,22},{7,23},{8,24},{9,... | collective-permute-start | bytes 98312 | tf_op jit(solution)/shard_map/ppermute | solution.py:31
  223.7 8.8 %collective-permute-start.22 = (f32[4,1,16,128]{3,2,1,0:T(8,128)S(1)}, f32[4,1,16,128]{3,2,1,0:T(8,128)S(1)}, u32[]{:S(2)}, u32[]{:S(2)}) collective-permute-start(f32[4,1,16,128]{3,2,1,0:T(8,128)S(1)} %get-tuple-element.32), channel_id=1, source_target_pairs={{16,0},{17,1},{18,2},{19,3},{20,4},{21,5},{22,6},{23,7},{24,8},{25... | collective-permute-start | bytes 98312 | tf_op jit(solution)/shard_map/ppermute | solution.py:33
  225.8 15.3 %all-to-all-start.1 = ((f32[32,1,192]{2,1,0:T(1,128)}), f32[32,1,192]{2,1,0:T(1,128)S(1)}, u32[]{:S(2)}, u32[]{:S(2)}) async-start(f32[32,1,192]{2,1,0:T(1,128)} %reshape.191), calls=%async_computation.1 | async-start | bytes 65536 | tf_op jit(solution)/shard_map/all_to_all | solution.py:82
  232.5 235.2 %reduce-scatter.3.cloned.1.call-start = ((), (), s32[]{:S(2)}) async-start(), calls=%async_computation.6 | async-start | bytes 17825792 | tf_op jit(solution)/shard_map/reduce_scatter | solution.py:86
  232.5 2.3 copy-start.14
  232.6 2.3 copy-start.16
  232.7 9.2 %collective-permute-start.23 = (f32[4,18,1,128]{3,1,2,0:T(8,128)S(1)}, f32[4,18,1,128]{3,1,2,0:T(8,128)S(1)}, u32[]{:S(2)}, u32[]{:S(2)}) collective-permute-start(f32[4,18,1,128]{3,1,2,0:T(8,128)S(1)} %copy.216), channel_id=1, source_target_pairs={{0,4},{4,8},{8,12},{1,5},{5,9},{9,13},{2,6},{6,10},{10,14},{3,7},{... | collective-permute-start | bytes 110600 | tf_op jit(solution)/shard_map/ppermute | solution.py:31
  234.9 11.3 %collective-permute-start.24 = (f32[4,18,1,128]{3,1,2,0:T(8,128)S(1)}, f32[4,18,1,128]{3,1,2,0:T(8,128)S(1)}, u32[]{:S(2)}, u32[]{:S(2)}) collective-permute-start(f32[4,18,1,128]{3,1,2,0:T(8,128)S(1)} %copy.217), channel_id=1, source_target_pairs={{4,0},{8,4},{12,8},{5,1},{9,5},{13,9},{6,2},{10,6},{14,10},{7,3},{... | collective-permute-start | bytes 110600 | tf_op jit(solution)/shard_map/ppermute | solution.py:33
  258.7 2.7 copy-start
  261.4 28.5 %collective-permute-start.25 = (f32[4,18,18,1]{2,1,3,0:T(8,128)S(1)}, f32[4,18,18,1]{2,1,3,0:T(8,128)S(1)}, u32[]{:S(2)}, u32[]{:S(2)}) collective-permute-start(f32[4,18,18,1]{2,1,3,0:T(8,128)S(1)} %get-tuple-element.23), channel_id=1, source_target_pairs={{0,1},{1,2},{2,3},{4,5},{5,6},{6,7},{8,9},{9,10},{10,11},{12,13},{... | collective-permute-start | bytes 15560 | tf_op jit(solution)/shard_map/ppermute | solution.py:31
  264.9 25.6 %collective-permute-start.26 = (f32[4,18,18,1]{2,1,3,0:T(8,128)S(1)}, f32[4,18,18,1]{2,1,3,0:T(8,128)}, u32[]{:S(2)}, u32[]{:S(2)}) collective-permute-start(f32[4,18,18,1]{2,1,3,0:T(8,128)S(1)} %get-tuple-element.24), channel_id=1, source_target_pairs={{1,0},{2,1},{3,2},{5,4},{6,5},{7,6},{9,8},{10,9},{11,10},{13,12},{... | collective-permute-start | bytes 15560 | tf_op jit(solution)/shard_map/ppermute | solution.py:33
  497.8 3.9 collective-permute-start.27
  501.7 5.4 collective-permute-start.28
  507.2 6.0 collective-permute-start.29
  513.2 6.0 collective-permute-start.30
  519.2 6.0 collective-permute-start.31
  525.3 6.0 collective-permute-start.32
  531.3 6.2 collective-permute-start.33
  537.5 6.2 collective-permute-start.34
  543.7 6.0 collective-permute-start.35
  549.7 6.0 collective-permute-start.36
  555.8 6.0 collective-permute-start.37
  561.8 6.0 collective-permute-start.38
  567.9 6.2 collective-permute-start.39
  574.1 6.2 collective-permute-start.40
  580.2 6.2 collective-permute-start.41
  587.4 27.4 %copy-start.3 = (f32[4,16,16,128]{3,2,1,0:T(8,128)S(1)}, f32[4,16,16,128]{3,2,1,0:T(8,128)}, u32[]{:S(2)}) copy-start(f32[4,16,16,128]{3,2,1,0:T(8,128)} %get-tuple-element.15) | copy-start | bytes 1572868
  609.9 25.2 %all-to-all-start.2 = ((f32[32,1,256]{2,1,0:T(1,128)}), f32[32,1,256]{2,1,0:T(1,128)S(1)}, u32[]{:S(2)}, u32[]{:S(2)}) async-start(f32[32,1,256]{2,1,0:T(1,128)} %reshape.193), calls=%async_computation.3 | async-start | bytes 65536 | tf_op jit(solution)/shard_map/all_to_all | solution.py:73
  614.8 8.7 copy-start.10
  636.8 13.1 %all-to-all-start.3 = ((f32[32,1,192]{2,1,0:T(1,128)}), f32[32,1,192]{2,1,0:T(1,128)S(1)}, u32[]{:S(2)}, u32[]{:S(2)}) async-start(f32[32,1,192]{2,1,0:T(1,128)} %reshape.195), calls=%async_computation.4 | async-start | bytes 65536 | tf_op jit(solution)/shard_map/all_to_all | solution.py:82
  642.7 200.9 %reduce-scatter.5.cloned.1.call-start = ((), (), s32[]{:S(2)}) async-start(), calls=%async_computation.7 | async-start | bytes 17825792 | tf_op jit(solution)/shard_map/reduce_scatter | solution.py:86
  (9 other events, 9.1 us)
Sparse Core Ops, SparseCore 0:
  285.4 182.2 reduce-scatter.2
  669.8 173.6 reduce-scatter.4
